TPU v7x, 256 devices: a whole 4x4x8 slice. The times are simulated.
256 devices in a mesh: row: 16 (over z, core), col: 16 (over x, y).
Axes of the slice: x: 4, y: 4, z: 8, core: 2. Of those that a mesh axis runs over, the one named last changes fastest.
Arguments:
- positions: float32 [3, 98304], P(None, ('row', 'col')), may hold values from -5 to 5
- velocities: float32 [3, 98304], P(None, ('row', 'col')), may hold values from -5 to 5
- accels: float32 [3, 98304], P(None, ('row', 'col')), may hold values from -12 to 12
- jerks: float32 [3, 98304], P(None, ('row', 'col')), may hold values from -6 to 6
- masses: float32 [98304], P(('row', 'col')), may hold values from 0.2 to 5
- star_time: float32 [98304], P(('row', 'col')), may hold values from -0.3 to 0
- block_steps: float32 [1], replicated, may hold values from 0.1 to 0.3
- act_index: int32 [1, 32768], P(None, ('row', 'col')), may hold values from 0 to 383, as said below
- act_count: int32 [1, 256], P(None, ('row', 'col')), may hold values from 1 to 128, 8192 in all within a row
Outputs:
- new_positions: float32 [3, 98304], P(None, ('row', 'col'))
- new_velocities: float32 [3, 98304], P(None, ('row', 'col'))
- new_accels: float32 [3, 98304], P(None, ('row', 'col'))
- new_jerks: float32 [3, 98304], P(None, ('row', 'col'))
Inputs may be any that keep to these rules, and one draw needn't show every extreme that they name: `act_index`: in each block step the 128 entries of one device are distinct local star numbers of that device; only the first act_count entries are active. Each row of act_count is one block step; its entries, one for each device, sum to 32 times the number of devices over all devices together.
All inputs are finite; a program needn't handle non-finite values.
Results may differ from a plain program's by a relative error of at most 0.00017.
Values sent between devices are 32-bit elements; how exact they have to be, the bound alone decides.
A program may use at most 64 MiB of HBM per device.

v0:
```python
import math

import jax
import jax.numpy as jnp
from jax import lax
from jax.sharding import PartitionSpec as P

SOFTENING = 0.0025
GRAVITY = 8.0


def predict(positions, velocities, accels, jerks, elapsed):
    square = elapsed * elapsed
    pred_pos = (
        positions
        + velocities * elapsed
        + accels * (square * 0.5)
        + jerks * (square * elapsed / 6.0)
    )
    pred_vel = velocities + accels * elapsed + jerks * (square * 0.5)
    return (pred_pos, pred_vel)


def pair_forces(target_pos, target_vel, source_pos, source_vel, source_mass, strength):
    separation = source_pos[:, None, :] - target_pos[:, :, None]
    relvel = source_vel[:, None, :] - target_vel[:, :, None]
    soft_sq = jnp.sum(separation * separation, axis=0) + SOFTENING
    inverse = lax.rsqrt(soft_sq)
    weight = (source_mass * strength)[None, :] * inverse * inverse * inverse
    radial = jnp.sum(separation * relvel, axis=0)
    factor = 3.0 * radial / soft_sq * weight
    accel = jnp.sum(weight[None] * separation, axis=2)
    jerk = jnp.sum(weight[None] * relvel - factor[None] * separation, axis=2)
    return jnp.concatenate([accel, jerk], axis=0)


def blocked_forces(target_pos, target_vel, source_pos, source_vel, source_mass, strength):
    total = target_pos.shape[1]
    block_len = math.gcd(512, total)
    nblocks = total // block_len
    pos_blocks = target_pos.reshape(3, nblocks, block_len).transpose(1, 0, 2)
    vel_blocks = target_vel.reshape(3, nblocks, block_len).transpose(1, 0, 2)
    result = lax.map(
        lambda target_pair: pair_forces(
            target_pair[0], target_pair[1], source_pos, source_vel, source_mass, strength
        ),
        (pos_blocks, vel_blocks),
    )
    return result.transpose(1, 0, 2).reshape(6, total)


def correct(pred_pos, pred_vel, old_acc, old_jerk, new_acc, new_jerk, span):
    change = old_acc - new_acc
    snap_term = -6.0 * change - span * (4.0 * old_jerk + 2.0 * new_jerk)
    crack_term = 12.0 * change + 6.0 * span * (old_jerk + new_jerk)
    out_pos = pred_pos + span * span * (snap_term / 24.0 + crack_term / 120.0)
    out_vel = pred_vel + span * (snap_term / 6.0 + crack_term / 24.0)
    return (out_pos, out_vel)


def collect(packet):
    partial_cols = lax.all_gather(packet, "col", axis=1, tiled=True)
    return lax.all_gather(partial_cols, "row", axis=1, tiled=True)


def distribute(forces):
    partial_sums = lax.psum_scatter(forces, "row", scatter_dimension=1, tiled=True)
    return lax.psum_scatter(partial_sums, "col", scatter_dimension=1, tiled=True)


def per_device(
    positions, velocities, accels, jerks, masses, star_time, block_steps, act_index, act_count
):
    per_dev = positions.shape[1]
    capacity = act_index.shape[1]
    devices = lax.axis_size("row") * lax.axis_size("col")
    strength = GRAVITY / (per_dev * devices)
    slot_ids = jnp.arange(capacity, dtype=jnp.int32)
    clock = jnp.float32(0.0)
    clock = block_steps[0]
    pred_pos, pred_vel = predict(positions, velocities, accels, jerks, clock - star_time)
    indices = act_index[0]
    active = slot_ids < act_count[0, 0]
    mine_pos = pred_pos[:, indices]
    mine_vel = pred_vel[:, indices]
    packet = jnp.concatenate([mine_pos, mine_vel, active.astype(jnp.float32)[None, :]], axis=0)
    gathered = collect(packet)
    forces = blocked_forces(gathered[:3], gathered[3:6], pred_pos, pred_vel, masses, strength)
    own_forces = distribute(forces)
    new_acc = own_forces[:3]
    new_jerk = own_forces[3:]
    span = clock - star_time[indices]
    out_pos, out_vel = correct(
        mine_pos, mine_vel, accels[:, indices], jerks[:, indices], new_acc, new_jerk, span
    )
    write_cols = jnp.where(active, indices, per_dev)
    positions = positions.at[:, write_cols].set(out_pos, mode="drop")
    velocities = velocities.at[:, write_cols].set(out_vel, mode="drop")
    accels = accels.at[:, write_cols].set(new_acc, mode="drop")
    jerks = jerks.at[:, write_cols].set(new_jerk, mode="drop")
    return (positions, velocities, accels, jerks)


def solution(mesh):
    in_specs = (
        P(None, ("row", "col")),
        P(None, ("row", "col")),
        P(None, ("row", "col")),
        P(None, ("row", "col")),
        P(("row", "col")),
        P(("row", "col")),
        P(),
        P(None, ("row", "col")),
        P(None, ("row", "col")),
    )
    out_specs = (
        P(None, ("row", "col")),
        P(None, ("row", "col")),
        P(None, ("row", "col")),
        P(None, ("row", "col")),
    )
    return jax.shard_map(
        per_device, mesh=mesh, in_specs=in_specs, out_specs=out_specs, check_vma=False
    )
```

profile of v0, /device:TPU:1, one launch (start us, length us, event | category | flops | bytes accessed | tf_op | source)
XLA Modules:
  0.0 350.3 jit_solution(3526304197783854758)
XLA Ops:
  12.4 19.3 %all_gather.6 = f32[7,2048]{1,0:T(8,128)S(1)} all-gather(f32[7,128]{1,0:T(8,128)S(1)} %pad_maximum_fusion), channel_id=1, replica_groups=mesh['row'=16,'col'=16] {'col'}, dimensions={1}, use_global_device_ids=true | all-gather | bytes 60928 | tf_op jit(solution)/shard_map/all_gather | solution.py:62
  31.8 28.9 %all_gather.7 = f32[7,32768]{1,0:T(8,128)S(1)} all-gather(f32[7,2048]{1,0:T(8,128)S(1)} %all_gather.6), channel_id=1, replica_groups=mesh['row'=16,'col'=16] {'row'}, dimensions={1}, use_global_device_ids=true | all-gather | bytes 974848 | tf_op jit(solution)/shard_map/all_gather | solution.py:63
  61.3 142.9 %while.10 = (s32[]{:T(128)}, f32[64,6,512]{2,1,0:T(8,128)S(1)}, f32[384]{0:T(512)S(1)}, f32[3,384]{1,0:T(4,128)S(1)}, f32[64,3,512]{2,1,0:T(4,128)S(1)}, /*index...) while((s32[]{:T(128)}, f32[64,6,512]{2,1,0:T(8,128)S(1)}, f32[384]{0:T(512)S(1)}, ...), condition=%wide.region_5.6_spmd, body=%wide.region_0.5_spmd.sunk | while | flops 9240962 | bytes 6408797 | solution.py:43
  62.1 1.4 fusion.22
  64.3 1.4 fusion.22
  66.6 1.4 fusion.22
  68.8 1.4 fusion.22
  71.0 1.4 fusion.22
  73.3 1.4 fusion.22
  75.5 1.4 fusion.22
  77.7 1.4 fusion.22
  80.0 1.4 fusion.22
  82.2 1.4 fusion.22
  84.4 1.4 fusion.22
  86.7 1.4 fusion.22
  88.9 1.4 fusion.22
  91.1 1.4 fusion.22
  93.4 1.4 fusion.22
  95.6 1.4 fusion.22
  97.8 1.4 fusion.22
  100.1 1.4 fusion.22
  102.3 1.4 fusion.22
  104.5 1.4 fusion.22
  106.8 1.4 fusion.22
  109.0 1.4 fusion.22
  111.2 1.4 fusion.22
  113.5 1.4 fusion.22
  115.7 1.4 fusion.22
  117.9 1.4 fusion.22
  120.2 1.4 fusion.22
  122.4 1.4 fusion.22
  124.6 1.4 fusion.22
  126.9 1.4 fusion.22
  129.1 1.4 fusion.22
  131.3 1.4 fusion.22
  133.6 1.4 fusion.22
  135.8 1.4 fusion.22
  138.0 1.4 fusion.22
  140.3 1.4 fusion.22
  142.5 1.4 fusion.22
  144.7 1.4 fusion.22
  147.0 1.4 fusion.22
  149.2 1.4 fusion.22
  151.4 1.4 fusion.22
  171.5 1.4 fusion.22
  187.1 1.4 fusion.22
  206.6 49.4 %reduce-scatter.3.cloned.1.call-done = f32[6,2048]{1,0:T(8,128)} async-done(((f32[6,32768]{1,0:T(8,128)}), f32[6,2048]{1,0:T(8,128)}) %reduce-scatter.3.cloned.1.call-update) | async-done | bytes 49168 | tf_op jit(solution)/shard_map/reduce_scatter | solution.py:67
  258.0 77.4 %reduce-scatter.5.cloned.1.call-done = f32[6,128]{1,0:T(8,128)} async-done(((f32[6,2048]{1,0:T(8,128)}), f32[6,128]{1,0:T(8,128)}) %reduce-scatter.5.cloned.1.call-update) | async-done | bytes 3088 | tf_op jit(solution)/shard_map/reduce_scatter | solution.py:68
  (399 shorter events, 96.4 us)
Async XLA Ops:
  7.2 248.8 %reduce-scatter.3.cloned.1.call-start = ((), (), s32[]{:S(2)}) async-start(), calls=%async_computation.2 | async-start | bytes 1114112 | tf_op jit(solution)/shard_map/reduce_scatter | solution.py:67
  60.6 0.7 copy-start.2
  204.2 1.0 copy-start.1
  204.2 1.1 copy-start
  204.2 51.8 %copy-start.3 = (f32[3,384]{1,0:T(4,128)S(1)}, f32[3,384]{1,0:T(4,128)}, u32[]{:S(2)}) copy-start(f32[3,384]{1,0:T(4,128)} %param.13) | copy-start | bytes 13828
  204.2 51.9 %copy-start.4 = (f32[3,384]{1,0:T(4,128)S(1)}, f32[3,384]{1,0:T(4,128)}, u32[]{:S(2)}) copy-start(f32[3,384]{1,0:T(4,128)} %param.14) | copy-start | bytes 13828
  204.2 52.0 %copy-start.5 = (f32[3,384]{1,0:T(4,128)S(1)}, f32[3,384]{1,0:T(4,128)}, u32[]{:S(2)}) copy-start(f32[3,384]{1,0:T(4,128)} %param.12) | copy-start | bytes 13828
  204.3 52.2 %copy-start.6 = (f32[3,384]{1,0:T(4,128)S(1)}, f32[3,384]{1,0:T(4,128)}, u32[]{:S(2)}) copy-start(f32[3,384]{1,0:T(4,128)} %param.11) | copy-start | bytes 13828
  205.2 130.3 %reduce-scatter.5.cloned.1.call-start = ((), (), s32[]{:S(2)}) async-start(), calls=%async_computation.3 | async-start | bytes 69632 | tf_op jit(solution)/shard_map/reduce_scatter | solution.py:68
Sparse Core Ops, SparseCore 0:
  205.3 50.5 reduce-scatter.2
  259.4 76.0 reduce-scatter.4
where the time goes:
time: 351 us; the launch traced here: 350 us
  other arithmetic  142 us (40%)
  waiting for transfers between devices  127 us (36%)
  blocking collectives  48.2 us (14%)
  between operations  15.6 us (4%)
  local copies, waits for them, and re-layouts  14.4 us (4%)
    reduce_sum x64, other arithmetic, pair_forces(): accel = jnp.sum(weight[None] * separation, axis=2)  89.4 us
    reduce_scatter x1, waiting for transfers between devices, distribute(): lax.psum_scatter(partial_sums, 'col', scatter_dimension=1, tiled=True)  77.4 us
    reduce_scatter x1, waiting for transfers between devices, distribute(): lax.psum_scatter(forces, 'row', scatter_dimension=1, tiled=True)  49.4 us
    reduce_sum x64, other arithmetic, pair_forces(): soft_sq = jnp.sum(separation * separation, axis=0) + SOFTENING  33.2 us
    all_gather x1, blocking collectives, collect(): return lax.all_gather(partial_cols, 'row', axis=1, tiled=True)  28.9 us
    all_gather x1, blocking collectives, collect(): partial_cols = lax.all_gather(packet, 'col', axis=1, tiled=True)  19.3 us
    mul x64, other arithmetic, pair_forces(): factor = 3.0 * radial / soft_sq * weight  15.5 us
  transfers between devices with their start and end apart: 2, of which 2 were waited for; matrix products, arithmetic and copies ran while one was open for 1% of the time, Pallas kernels for 0%

commit v1 on v0

v1 whole, which is shorter than its diff:
```python
import functools

import jax
import jax.numpy as jnp
from jax import lax
from jax.experimental import pallas as pl
from jax.experimental.pallas import tpu as pltpu
from jax.sharding import PartitionSpec as P

SOFTENING = 0.0025
GRAVITY = 8.0
LANES = 128
ROWS = 2
MESH = pl.DeviceIdType.MESH
HIGHEST = lax.Precision.HIGHEST


def predict(pos, vel, acc, jerk, elapsed):
    square = elapsed * elapsed
    pred_pos = pos + vel * elapsed + acc * (square * 0.5) + jerk * (square * elapsed / 6.0)
    pred_vel = vel + acc * elapsed + jerk * (square * 0.5)
    return pred_pos, pred_vel


def peer_a(k, n_col):
    group = ROWS * n_col
    row, col = lax.axis_index("row"), lax.axis_index("col")
    mine = (row % ROWS) * n_col + col
    other = (mine + k) % group
    return (row // ROWS) * ROWS + other // n_col, other % n_col


def peer_b(k, n_row):
    group = n_row // ROWS
    row, col = lax.axis_index("row"), lax.axis_index("col")
    return ((row // ROWS + k) % group) * ROWS + row % ROWS, col


def one_hot(index_row, count, stars):
    star = lax.broadcasted_iota(jnp.int32, (stars, LANES), 0)
    slot = lax.broadcasted_iota(jnp.int32, (stars, LANES), 1)
    return jnp.where((star == index_row) & (slot < count), 1.0, 0.0)


def exchange_kernel(
    n_row, n_col, strength,
    step_ref, count_ref, pos_ref, vel_ref, acc_ref, jerk_ref, mass_ref, time_ref, index_ref,
    tgt_ref, src_ref, cnt_ref,
    send_a, recv_a, send_b, recv_b,
):
    n_a, n_b = ROWS * n_col, n_row // ROWS
    barrier = pltpu.get_barrier_semaphore()

    def greet_a(k, _):
        pl.semaphore_signal(barrier, inc=1, device_id=peer_a(k, n_col), device_id_type=MESH)
        return 0

    def greet_b(k, _):
        pl.semaphore_signal(barrier, inc=1, device_id=peer_b(k, n_row), device_id_type=MESH)
        return 0

    lax.fori_loop(1, n_a, greet_a, 0)
    lax.fori_loop(1, n_b, greet_b, 0)

    stars = pos_ref.shape[1]
    elapsed = step_ref[0] - time_ref[...].reshape(1, stars)
    pred_pos, pred_vel = predict(pos_ref[...], vel_ref[...], acc_ref[...], jerk_ref[...], elapsed)
    weight = mass_ref[...].reshape(1, stars) * strength
    packet = jnp.concatenate([pred_pos, pred_vel, weight, jnp.zeros_like(weight)], axis=0)
    src_ref[0] = packet
    count = count_ref[0, 0]
    chosen = jnp.dot(
        packet, one_hot(index_ref[...], LANES, stars), precision=HIGHEST,
        preferred_element_type=jnp.float32,
    )
    comp = lax.broadcasted_iota(jnp.int32, (8, LANES), 0)
    tgt_ref[0] = jnp.where(comp == 6, count.astype(jnp.float32), chosen)

    pl.semaphore_wait(barrier, n_a + n_b - 2)

    def copy_b(k):
        return pltpu.make_async_remote_copy(
            src_ref=src_ref.at[0], dst_ref=src_ref.at[n_b - k],
            send_sem=send_b.at[k], recv_sem=recv_b.at[n_b - k],
            device_id=peer_b(k, n_row), device_id_type=MESH,
        )

    def copy_a(k):
        return pltpu.make_async_remote_copy(
            src_ref=tgt_ref.at[0], dst_ref=tgt_ref.at[n_a - k],
            send_sem=send_a.at[k], recv_sem=recv_a.at[n_a - k],
            device_id=peer_a(k, n_col), device_id_type=MESH,
        )

    def start_b(k, _):
        copy_b(k).start()
        return 0

    def start_a(k, _):
        copy_a(k).start()
        return 0

    def wait_b(k, _):
        copy_b(k).wait()
        return 0

    def wait_a(k, _):
        copy_a(k).wait()
        return 0

    lax.fori_loop(1, n_b, start_b, 0)
    lax.fori_loop(1, n_a, start_a, 0)
    lax.fori_loop(1, n_a, wait_a, 0)
    lane = lax.broadcasted_iota(jnp.int32, (1, LANES), 1)
    counts = jnp.zeros((1, LANES), jnp.float32)
    for k in range(n_a):
        counts = jnp.where(lane == k, tgt_ref[k, 6:7, :], counts)
    cnt_ref[...] = counts.astype(jnp.int32)
    lax.fori_loop(1, n_b, wait_b, 0)


def force_kernel(cnt_ref, tgt_ref, src_ref, out_ref, dense, dense_t, res_t, srcb, offs):
    n_a, n_b, stars = tgt_ref.shape[0], src_ref.shape[0], src_ref.shape[2]
    per = stars // LANES
    chunks = n_b * per

    for b in range(n_b):
        for p in range(per):
            for c in range(7):
                row = src_ref[b, c : c + 1, p * LANES : (p + 1) * LANES]
                srcb[c, b * per + p] = jnp.broadcast_to(row, (8, LANES))

    lane = lax.broadcasted_iota(jnp.int32, (8, LANES), 1)

    def compact(k, off):
        tile, shift = off // LANES, off % LANES
        rolled = pltpu.roll(tgt_ref[k], shift, 1)
        dense[tile] = jnp.where(lane >= shift, rolled, dense[tile])
        dense[tile + 1] = rolled
        offs[k] = off
        return off + cnt_ref[0, k]

    total = lax.fori_loop(0, n_a, compact, jnp.int32(0))
    tiles = (total + LANES - 1) // LANES

    def turn(t, _):
        dense_t[pl.ds(pl.multiple_of(t * LANES, LANES), LANES), 0:8] = dense[t].T
        return 0

    lax.fori_loop(0, tiles, turn, 0)
    blocks = (total + 15) // 16

    def block(i, _):
        base = pl.multiple_of(i * 16, 16)
        own = []
        for h in range(2):
            rows = dense_t[pl.ds(base + 8 * h, 8), :]
            own.append([jnp.broadcast_to(rows[:, c : c + 1], (8, LANES)) for c in range(6)])
        sums = [[jnp.zeros((8, LANES), jnp.float32) for _ in range(6)] for _ in range(2)]
        for j in range(chunks):
            s = [srcb[c, j] for c in range(7)]
            for h in range(2):
                d = [s[c] - own[h][c] for c in range(6)]
                q = d[0] * d[0] + d[1] * d[1] + d[2] * d[2] + SOFTENING
                inv = lax.rsqrt(q)
                inv2 = inv * inv
                w = s[6] * inv * inv2
                radial = d[0] * d[3] + d[1] * d[4] + d[2] * d[5]
                f = (3.0 * radial) * inv2
                for c in range(3):
                    wr = w * d[c]
                    sums[h][c] = sums[h][c] + wr
                    sums[h][3 + c] = sums[h][3 + c] + (w * d[3 + c] - f * wr)
        for h in range(2):
            res = jnp.zeros((8, LANES), jnp.float32)
            for c in range(6):
                res = jnp.where(lane == c, jnp.sum(sums[h][c], axis=1, keepdims=True), res)
            res_t[pl.ds(base + 8 * h, 8), :] = res
        return 0

    lax.fori_loop(0, blocks, block, 0)

    def back(t, _):
        dense[t] = res_t[pl.ds(pl.multiple_of(t * LANES, LANES), LANES), :].T[0:8]
        return 0

    lax.fori_loop(0, tiles, back, 0)

    def spread(k, _):
        off = offs[k]
        tile, shift = off // LANES, off % LANES
        both = jnp.where(lane >= shift, dense[tile], dense[tile + 1])
        out_ref[k] = pltpu.roll(both, (LANES - shift) % LANES, 1)
        return 0

    lax.fori_loop(0, n_a, spread, 0)


def return_kernel(
    n_row, n_col,
    step_ref, count_ref, part_ref, pos_ref, vel_ref, acc_ref, jerk_ref, time_ref, index_ref,
    new_pos, new_vel, new_acc, new_jerk,
    inbox, send_sem, recv_sem,
):
    n_a = ROWS * n_col
    barrier = pltpu.get_barrier_semaphore()

    def greet(k, _):
        pl.semaphore_signal(barrier, inc=1, device_id=peer_a(k, n_col), device_id_type=MESH)
        return 0

    lax.fori_loop(1, n_a, greet, 0)
    stars = pos_ref.shape[1]
    clock = step_ref[0]
    span = clock - time_ref[...].reshape(1, stars)
    pos, vel, acc, jerk = pos_ref[...], vel_ref[...], acc_ref[...], jerk_ref[...]
    pred_pos, pred_vel = predict(pos, vel, acc, jerk, span)
    pick = one_hot(index_ref[...], count_ref[0, 0], stars)
    pl.semaphore_wait(barrier, n_a - 1)

    def copy(k):
        return pltpu.make_async_remote_copy(
            src_ref=part_ref.at[k], dst_ref=inbox.at[n_a - k],
            send_sem=send_sem.at[k], recv_sem=recv_sem.at[n_a - k],
            device_id=peer_a(k, n_col), device_id_type=MESH,
        )

    def start(k, _):
        copy(k).start()
        return 0

    def wait(k, _):
        copy(k).wait()
        return 0

    lax.fori_loop(1, n_a, start, 0)
    lax.fori_loop(1, n_a, wait, 0)
    total = part_ref[0]
    for k in range(1, n_a):
        total = total + inbox[k]
    comp = lax.broadcasted_iota(jnp.int32, (8, LANES), 0)
    total = jnp.where(comp < 6, total, 1.0)
    placed = lax.dot_general(
        total, pick, (((1,), (1,)), ((), ())), precision=HIGHEST,
        preferred_element_type=jnp.float32,
    )
    active = placed[6:7] > 0.5
    acc1, jerk1 = placed[0:3], placed[3:6]
    change = acc - acc1
    snap = -6.0 * change - span * (4.0 * jerk + 2.0 * jerk1)
    crack = 12.0 * change + 6.0 * span * (jerk + jerk1)
    out_pos = pred_pos + span * span * (snap / 24.0 + crack / 120.0)
    out_vel = pred_vel + span * (snap / 6.0 + crack / 24.0)
    new_pos[...] = jnp.where(active, out_pos, pos)
    new_vel[...] = jnp.where(active, out_vel, vel)
    new_acc[...] = jnp.where(active, acc1, acc)
    new_jerk[...] = jnp.where(active, jerk1, jerk)


def solution(mesh):
    n_row, n_col = mesh.shape["row"], mesh.shape["col"]
    n_a, n_b = ROWS * n_col, n_row // ROWS
    vmem = pl.BlockSpec(memory_space=pltpu.VMEM)
    smem = pl.BlockSpec(memory_space=pltpu.SMEM)
    f32 = jnp.float32

    def per_device(pos, vel, acc, jerk, mass, time, steps, index, count):
        stars = pos.shape[1]
        strength = GRAVITY / (stars * n_row * n_col)
        tgt, src, cnt = pl.pallas_call(
            functools.partial(exchange_kernel, n_row, n_col, strength),
            out_shape=(
                jax.ShapeDtypeStruct((n_a, 8, LANES), f32),
                jax.ShapeDtypeStruct((n_b, 8, stars), f32),
                jax.ShapeDtypeStruct((1, LANES), jnp.int32),
            ),
            in_specs=[smem, smem] + [vmem] * 7,
            out_specs=(vmem, vmem, vmem),
            scratch_shapes=[
                pltpu.SemaphoreType.DMA((n_a,)),
                pltpu.SemaphoreType.DMA((n_a,)),
                pltpu.SemaphoreType.DMA((n_b,)),
                pltpu.SemaphoreType.DMA((n_b,)),
            ],
            compiler_params=pltpu.CompilerParams(collective_id=0, has_side_effects=True),
            name="exchange",
        )(steps, count, pos, vel, acc, jerk, mass, time, index)
        chunks = n_b * stars // LANES
        part = pl.pallas_call(
            force_kernel,
            out_shape=jax.ShapeDtypeStruct((n_a, 8, LANES), f32),
            in_specs=[smem, vmem, vmem],
            out_specs=vmem,
            scratch_shapes=[
                pltpu.VMEM((n_a + 2, 8, LANES), f32),
                pltpu.VMEM(((n_a + 2) * LANES, LANES), f32),
                pltpu.VMEM(((n_a + 2) * LANES, LANES), f32),
                pltpu.VMEM((7, chunks, 8, LANES), f32),
                pltpu.SMEM((n_a,), jnp.int32),
            ],
            name="forces",
        )(cnt, tgt, src)
        return pl.pallas_call(
            functools.partial(return_kernel, n_row, n_col),
            out_shape=(jax.ShapeDtypeStruct(pos.shape, f32),) * 4,
            in_specs=[smem, smem] + [vmem] * 7,
            out_specs=(vmem,) * 4,
            scratch_shapes=[
                pltpu.VMEM((n_a, 8, LANES), f32),
                pltpu.SemaphoreType.DMA((n_a,)),
                pltpu.SemaphoreType.DMA((n_a,)),
            ],
            compiler_params=pltpu.CompilerParams(collective_id=1, has_side_effects=True),
            name="returns",
        )(steps, count, part, pos, vel, acc, jerk, time, index)

    both = ("row", "col")
    state = P(None, both)
    return jax.shard_map(
        per_device,
        mesh=mesh,
        in_specs=(state, state, state, state, P(both), P(both), P(), state, state),
        out_specs=(state, state, state, state),
        check_vma=False,
    )
```

time: 351 us -> 74.6 us (0.21)
  other arithmetic: 142 us -> 0 us
  waiting for transfers between devices: 127 us -> 0 us
  Pallas kernels: 0 us -> 68.7 us
  blocking collectives: 48.2 us -> 0 us
  between operations: 15.6 us -> 1.95 us
  local copies, waits for them, and re-layouts: 14.4 us -> 3.36 us
    reduce_scatter x2 -> x0, waiting for transfers between devices: 127 us -> none  [the longest x1 77.4 us: distribute(): lax.psum_scatter(partial_sums, 'col', scatter_dimension=1, tiled=True)]
    reduce_sum x128 -> x0, other arithmetic: 123 us -> none  [the longest x64 89.4 us: pair_forces(): accel = jnp.sum(weight[None] * separation, axis=2)]
    pallas_call x0 -> x3, Pallas kernels: none -> 68.7 us  [the longest x1 38.2 us: per_device(): pl.pallas_call(force_kernel, out_shape=jax.ShapeDtypeStruct((n_a, 8, LANE...]
    all_gather x2 -> x0, blocking collectives: 48.2 us -> none  [the longest x1 28.9 us: collect(): return lax.all_gather(partial_cols, 'row', axis=1, tiled=True)]
    mul x131 -> x0, other arithmetic: 16.4 us -> none  [the longest x64 15.5 us: pair_forces(): factor = 3.0 * radial / soft_sq * weight]
    gather x9 -> x0, local copies, waits for them, and re-layouts: 4.11 us -> none  [the longest x1 1.27 us: per_device(): span = clock - star_time[indices]]
    scatter x4 -> x0, local copies, waits for them, and re-layouts: 3.89 us -> none  [the longest x1 0.97 us: per_device(): velocities = velocities.at[:, write_cols].set(out_vel, mode='drop')]
  transfers between devices with their start and end apart: 2 -> 0, of which waited for: 2 -> 0; matrix products, arithmetic and copies ran while one was open for 1% -> 0% of each run, Pallas kernels for 0% -> 0%
where the time goes in v1:
time: 74.6 us; the launch traced here: 74 us
  Pallas kernels  68.7 us (92%)
  local copies, waits for them, and re-layouts  3.36 us (5%)
  between operations  1.95 us (3%)
    pallas_call x1, Pallas kernels, per_device(): pl.pallas_call(force_kernel, out_shape=jax.ShapeDtypeStruct((n_a, 8, LANE...  38.2 us
    pallas_call x1, Pallas kernels, per_device(): pl.pallas_call(functools.partial(exchange_kernel, n_row, n_col, strength)...  18.9 us
    pallas_call x1, Pallas kernels, per_device(): pl.pallas_call(functools.partial(return_kernel, n_row, n_col), out_shape=...  11.5 us
    unnamed x12, local copies, waits for them, and re-layouts  3.36 us

profile of v1, /device:TPU:1, one launch (start us, length us, event | category | flops | bytes accessed | tf_op | source)
XLA Modules:
  0.0 74.0 jit_solution(13593949314136702560)
XLA Ops:
  1.9 18.9 %exchange.1 = (f32[32,8,128]{2,1,0:T(8,128)}, f32[8,8,384]{2,1,0:T(8,128)}, s32[1,128]{1,0:T(1,128)}) custom-call(f32[1]{0:T(128)S(6)} %copy.17.step_ref, s32[1,1]{1,0:T(1,128)S(6)} %copy.18.count_ref, f32[3,384]{1,0:T(4,128)} %pos_ref.3, f32[3,384]{1,0:T(4,128)} %vel_ref.3, f32[3,384]{1,0:T(4,128)} %acc_ref.3, f32[3,384]{1,0:T(4,128)} %jerk_ref.3, ...), custom_call_target="tpu_custom_call" | custom-call | tf_op jit(solution)/shard_map/exchange/pallas_call | solution.py:270
  20.8 38.2 %forces.1.part_ref = f32[32,8,128]{2,1,0:T(8,128)} custom-call(s32[1,128]{1,0:T(1,128)} %get-tuple-element.7.cnt_ref, f32[32,8,128]{2,1,0:T(8,128)} %get-tuple-element.8.tgt_ref, f32[8,8,384]{2,1,0:T(8,128)} %get-tuple-element.9.src_ref), custom_call_target="tpu_custom_call" | custom-call | tf_op jit(solution)/shard_map/forces/pallas_call | solution.py:289
  59.1 11.5 %returns.1 = (f32[3,384]{1,0:T(4,128)}, f32[3,384]{1,0:T(4,128)}, f32[3,384]{1,0:T(4,128)}, f32[3,384]{1,0:T(4,128)}) custom-call(f32[1]{0:T(128)S(6)} %copy.17.step_ref, s32[1,1]{1,0:T(1,128)S(6)} %copy.18.count_ref, f32[32,8,128]{2,1,0:T(8,128)} %forces.1.part_ref, f32[3,384]{1,0:T(4,128)} %pos_ref.3, f32[3,384]{1,0:T(4,128)} %vel_ref.3, ...), custom_call_target="tpu_custom_call" | custom-call | tf_op jit(solution)/shard_map/returns/pallas_call | solution.py:303
  70.6 0.0 copy-start.3
  70.6 0.7 copy-done.3
  71.3 0.0 copy-start.2
  71.3 0.6 copy.19
  71.9 0.1 copy-done.2
  72.0 0.0 copy-start.1
  72.0 0.6 copy.20
  72.6 0.1 copy-done.1
  72.7 0.0 copy-start
  72.7 0.6 copy.21
  73.3 0.1 copy-done
  73.4 0.6 copy.22
Async XLA Ops:
  70.6 0.7 copy-start.3
  71.3 0.7 copy-start.2
  72.0 0.7 copy-start.1
  72.7 0.7 copy-start

commit v2 on v1

--- a/solution.py
+++ b/solution.py
@@ -11,6 +11,7 @@
 GRAVITY = 8.0
 LANES = 128
 ROWS = 2
+AHEAD = 2
 MESH = pl.DeviceIdType.MESH
 HIGHEST = lax.Precision.HIGHEST
 
@@ -119,18 +120,54 @@
     lax.fori_loop(1, n_b, wait_b, 0)
 
 
-def force_kernel(cnt_ref, tgt_ref, src_ref, out_ref, dense, dense_t, res_t, srcb, offs):
+def split3(x):
+    high = x.astype(jnp.bfloat16).astype(jnp.float32)
+    rest = x - high
+    mid = rest.astype(jnp.bfloat16).astype(jnp.float32)
+    return high, mid, rest - mid
+
+
+def force_kernel(
+    cnt_ref, tgt_ref, src_ref, out_ref, dense, src_t, spot, packed, offs
+):
     n_a, n_b, stars = tgt_ref.shape[0], src_ref.shape[0], src_ref.shape[2]
     per = stars // LANES
-    chunks = n_b * per
-
-    for b in range(n_b):
-        for p in range(per):
-            for c in range(7):
-                row = src_ref[b, c : c + 1, p * LANES : (p + 1) * LANES]
-                srcb[c, b * per + p] = jnp.broadcast_to(row, (8, LANES))
-
+    parts = n_b * per
+    f32, bf16 = jnp.float32, jnp.bfloat16
+    comp = lax.broadcasted_iota(jnp.int32, (8, LANES), 0)
     lane = lax.broadcasted_iota(jnp.int32, (8, LANES), 1)
+    one = jnp.ones((1, LANES), f32)
+
+    def piece(j):
+        b, p = j // per, j % per
+        return src_ref[b, :, p * LANES : (p + 1) * LANES]
+
+    total = piece(0)
+    for j in range(1, parts):
+        total = total + piece(j)
+    middle = jnp.sum(total, axis=1, keepdims=True) * (1.0 / (parts * LANES))
+    middle = jnp.where(comp < 6, jnp.broadcast_to(middle, (8, LANES)), 0.0)
+
+    for j in range(parts):
+        state = piece(j) - middle
+        dot_xv = state[0:1] * state[3:4] + state[1:2] * state[4:5] + state[2:3] * state[5:6]
+        high, mid, low = split3(jnp.concatenate([state[3:6], state[0:3], dot_xv, one], axis=0))
+        rows = jnp.concatenate(
+            [high, mid, high, mid, low, high, state, jnp.zeros((8, LANES), f32)], axis=0
+        )
+        cols = rows.T
+        src_t[j * LANES : (j + 1) * LANES, :] = cols.astype(bf16)
+        for g in range(LANES // 8):
+            for c in range(3):
+                spot[j * (LANES // 8) + g, c] = jnp.broadcast_to(
+                    cols[8 * g : 8 * g + 8, 48 + c : 49 + c], (8, LANES)
+                )
+        mass = state[6:7]
+        moment = jnp.where(comp < 6, state * mass, jnp.where(comp == 6, state, 0.0))
+        high, mid, low = split3(moment)
+        rows = jnp.concatenate([high, mid, low, jnp.zeros((8, LANES), f32)], axis=0).astype(bf16)
+        packed[j, :, 0:LANES] = rows
+        packed[j, :, LANES : 2 * LANES] = rows
 
     def compact(k, off):
         tile, shift = off // LANES, off % LANES
@@ -140,51 +177,67 @@
         offs[k] = off
         return off + cnt_ref[0, k]
 
-    total = lax.fori_loop(0, n_a, compact, jnp.int32(0))
-    tiles = (total + LANES - 1) // LANES
-
-    def turn(t, _):
-        dense_t[pl.ds(pl.multiple_of(t * LANES, LANES), LANES), 0:8] = dense[t].T
-        return 0
-
-    lax.fori_loop(0, tiles, turn, 0)
-    blocks = (total + 15) // 16
-
-    def block(i, _):
-        base = pl.multiple_of(i * 16, 16)
-        own = []
-        for h in range(2):
-            rows = dense_t[pl.ds(base + 8 * h, 8), :]
-            own.append([jnp.broadcast_to(rows[:, c : c + 1], (8, LANES)) for c in range(6)])
-        sums = [[jnp.zeros((8, LANES), jnp.float32) for _ in range(6)] for _ in range(2)]
-        for j in range(chunks):
-            s = [srcb[c, j] for c in range(7)]
-            for h in range(2):
-                d = [s[c] - own[h][c] for c in range(6)]
-                q = d[0] * d[0] + d[1] * d[1] + d[2] * d[2] + SOFTENING
-                inv = lax.rsqrt(q)
-                inv2 = inv * inv
-                w = s[6] * inv * inv2
-                radial = d[0] * d[3] + d[1] * d[4] + d[2] * d[5]
-                f = (3.0 * radial) * inv2
-                for c in range(3):
-                    wr = w * d[c]
-                    sums[h][c] = sums[h][c] + wr
-                    sums[h][3 + c] = sums[h][3 + c] + (w * d[3 + c] - f * wr)
-        for h in range(2):
-            res = jnp.zeros((8, LANES), jnp.float32)
-            for c in range(6):
-                res = jnp.where(lane == c, jnp.sum(sums[h][c], axis=1, keepdims=True), res)
-            res_t[pl.ds(base + 8 * h, 8), :] = res
-        return 0
-
-    lax.fori_loop(0, blocks, block, 0)
-
-    def back(t, _):
-        dense[t] = res_t[pl.ds(pl.multiple_of(t * LANES, LANES), LANES), :].T[0:8]
-        return 0
-
-    lax.fori_loop(0, tiles, back, 0)
+    count = lax.fori_loop(0, n_a, compact, jnp.int32(0))
+    tiles = (count + LANES - 1) // LANES
+
+    def tile_step(t, _):
+        state = dense[t] - middle
+        dot_xv = state[0:1] * state[3:4] + state[1:2] * state[4:5] + state[2:3] * state[5:6]
+        high, mid, low = split3(jnp.concatenate([-state[0:6], one, dot_xv], axis=0))
+        pair = jnp.concatenate(
+            [high, high, mid, mid, high, low, jnp.zeros((16, LANES), f32)], axis=0
+        ).astype(bf16)
+        own = [jnp.broadcast_to(state[c : c + 1], (8, LANES)) for c in range(3)]
+
+        def radial_of(c):
+            return jnp.dot(
+                src_t[c * LANES : (c + 1) * LANES, :], pair, preferred_element_type=f32
+            )
+
+        def weights_of(c, radial):
+            tiles_of = [[], [], [], []]
+            for g in range(8):
+                pulls, twists = [], []
+                for h in range(2):
+                    at = c * 16 + 2 * g + h
+                    dx = spot[at, 0] - own[0]
+                    dy = spot[at, 1] - own[1]
+                    dz = spot[at, 2] - own[2]
+                    q = dx * dx + (dy * dy + (dz * dz + SOFTENING))
+                    inv = lax.rsqrt(q)
+                    inv2 = inv * inv
+                    pull = inv * inv2
+                    pulls.append(pull)
+                    twists.append((radial[16 * g + 8 * h : 16 * g + 8 * h + 8] * inv2) * pull)
+                for s, both in enumerate((pulls, twists)):
+                    full = jnp.concatenate(both, axis=0)
+                    high = full.astype(bf16)
+                    tiles_of[s].append(high)
+                    tiles_of[2 + s].append((full - high.astype(f32)).astype(bf16))
+            cols = [jnp.concatenate(x, axis=0) for x in tiles_of]
+            return jnp.concatenate(
+                [jnp.concatenate(cols[0:2], axis=1), jnp.concatenate(cols[2:4], axis=1)], axis=0
+            )
+
+        acc = jnp.zeros((32, 2 * LANES), f32)
+        ahead = [radial_of(c) for c in range(AHEAD)]
+        right = None
+        for c in range(parts):
+            if c + AHEAD < parts:
+                ahead.append(radial_of(c + AHEAD))
+            last, right = right, weights_of(c, ahead[c])
+            if last is not None:
+                acc = acc + jnp.dot(packed[c - 1], last, preferred_element_type=f32)
+        acc = acc + jnp.dot(packed[parts - 1], right, preferred_element_type=f32)
+        acc = acc[0:8] + (acc[8:16] + acc[16:24])
+        pull, twist = acc[:, :LANES], acc[:, LANES:]
+        force = pull - state * pull[6:7]
+        tide = twist - state * twist[6:7]
+        jerk = force[3:6] - 3.0 * tide[0:3]
+        dense[t] = jnp.concatenate([force[0:3], jerk, jnp.zeros((2, LANES), f32)], axis=0)
+        return 0
+
+    lax.fori_loop(0, tiles, tile_step, 0)
 
     def spread(k, _):
         off = offs[k]
@@ -293,9 +346,9 @@
             out_specs=vmem,
             scratch_shapes=[
                 pltpu.VMEM((n_a + 2, 8, LANES), f32),
-                pltpu.VMEM(((n_a + 2) * LANES, LANES), f32),
-                pltpu.VMEM(((n_a + 2) * LANES, LANES), f32),
-                pltpu.VMEM((7, chunks, 8, LANES), f32),
+                pltpu.VMEM((chunks * LANES, 64), jnp.bfloat16),
+                pltpu.VMEM((chunks * LANES // 8, 3, 8, LANES), f32),
+                pltpu.VMEM((chunks, 32, 2 * LANES), jnp.bfloat16),
                 pltpu.SMEM((n_a,), jnp.int32),
             ],
             name="forces",

time: 74.6 us -> 58 us (0.78)
  the two profiles are of different devices: /device:TPU:1 before, /device:TPU:33 now
where the time goes in v2:
time: 58 us; the launch traced here: 57.5 us
  Pallas kernels  52.2 us (90%)
  local copies, waits for them, and re-layouts  3.36 us (6%)
  between operations  1.95 us (3%)
    pallas_call x1, Pallas kernels, per_device(): pl.pallas_call(force_kernel, out_shape=jax.ShapeDtypeStruct((n_a, 8, LANE...  23.4 us
    pallas_call x1, Pallas kernels, per_device(): pl.pallas_call(functools.partial(exchange_kernel, n_row, n_col, strength)...  17.2 us
    pallas_call x1, Pallas kernels, per_device(): pl.pallas_call(functools.partial(return_kernel, n_row, n_col), out_shape=...  11.5 us
    unnamed x12, local copies, waits for them, and re-layouts  3.36 us

profile of v2, /device:TPU:33, one launch (start us, length us, event | category | flops | bytes accessed | tf_op | source)
XLA Modules:
  0.0 57.5 jit_solution(1942739371602163263)
XLA Ops:
  1.9 17.2 %exchange.1 = (f32[32,8,128]{2,1,0:T(8,128)}, f32[8,8,384]{2,1,0:T(8,128)}, s32[1,128]{1,0:T(1,128)}) custom-call(f32[1]{0:T(128)S(6)} %copy.17.step_ref, s32[1,1]{1,0:T(1,128)S(6)} %copy.18.count_ref, f32[3,384]{1,0:T(4,128)} %pos_ref.3, f32[3,384]{1,0:T(4,128)} %vel_ref.3, f32[3,384]{1,0:T(4,128)} %acc_ref.3, f32[3,384]{1,0:T(4,128)} %jerk_ref.3, ...), custom_call_target="tpu_custom_call" | custom-call | tf_op jit(solution)/shard_map/exchange/pallas_call | solution.py:323
  19.1 23.4 %forces.1.part_ref = f32[32,8,128]{2,1,0:T(8,128)} custom-call(s32[1,128]{1,0:T(1,128)} %get-tuple-element.7.cnt_ref, f32[32,8,128]{2,1,0:T(8,128)} %get-tuple-element.8.tgt_ref, f32[8,8,384]{2,1,0:T(8,128)} %get-tuple-element.9.src_ref), custom_call_target="tpu_custom_call" | custom-call | tf_op jit(solution)/shard_map/forces/pallas_call | solution.py:342
  42.6 11.5 %returns.1 = (f32[3,384]{1,0:T(4,128)}, f32[3,384]{1,0:T(4,128)}, f32[3,384]{1,0:T(4,128)}, f32[3,384]{1,0:T(4,128)}) custom-call(f32[1]{0:T(128)S(6)} %copy.17.step_ref, s32[1,1]{1,0:T(1,128)S(6)} %copy.18.count_ref, f32[32,8,128]{2,1,0:T(8,128)} %forces.1.part_ref, f32[3,384]{1,0:T(4,128)} %pos_ref.3, f32[3,384]{1,0:T(4,128)} %vel_ref.3, ...), custom_call_target="tpu_custom_call" | custom-call | tf_op jit(solution)/shard_map/returns/pallas_call | solution.py:356
  54.1 0.0 copy-start.3
  54.1 0.7 %copy-done.3 = f32[3,384]{1,0:T(4,128)S(1)} copy-done((f32[3,384]{1,0:T(4,128)S(1)}, f32[3,384]{1,0:T(4,128)}, u32[]{:S(2)}) %copy-start.3) | copy-done | bytes 4632
  54.8 0.0 copy-start.2
  54.8 0.6 %copy.19 = f32[3,384]{1,0:T(4,128)} copy(f32[3,384]{1,0:T(4,128)S(1)} %copy-done.3) | data formatting | bytes 9216
  55.4 0.1 copy-done.2
  55.5 0.0 copy-start.1
  55.5 0.6 %copy.20 = f32[3,384]{1,0:T(4,128)} copy(f32[3,384]{1,0:T(4,128)S(1)} %copy-done.2) | data formatting | bytes 9216
  56.1 0.1 copy-done.1
  56.2 0.0 copy-start
  56.2 0.6 %copy.21 = f32[3,384]{1,0:T(4,128)} copy(f32[3,384]{1,0:T(4,128)S(1)} %copy-done.1) | data formatting | bytes 9216
  56.8 0.1 copy-done
  56.9 0.6 %copy.22 = f32[3,384]{1,0:T(4,128)} copy(f32[3,384]{1,0:T(4,128)S(1)} %copy-done) | data formatting | bytes 9216
Async XLA Ops:
  54.1 0.7 %copy-start.3 = (f32[3,384]{1,0:T(4,128)S(1)}, f32[3,384]{1,0:T(4,128)}, u32[]{:S(2)}) copy-start(f32[3,384]{1,0:T(4,128)} %get-tuple-element.14) | copy-start | bytes 13828
  54.8 0.7 %copy-start.2 = (f32[3,384]{1,0:T(4,128)S(1)}, f32[3,384]{1,0:T(4,128)}, u32[]{:S(2)}) copy-start(f32[3,384]{1,0:T(4,128)} %get-tuple-element.15) | copy-start | bytes 13828
  55.5 0.7 %copy-start.1 = (f32[3,384]{1,0:T(4,128)S(1)}, f32[3,384]{1,0:T(4,128)}, u32[]{:S(2)}) copy-start(f32[3,384]{1,0:T(4,128)} %get-tuple-element.16) | copy-start | bytes 13828
  56.2 0.7 %copy-start = (f32[3,384]{1,0:T(4,128)S(1)}, f32[3,384]{1,0:T(4,128)}, u32[]{:S(2)}) copy-start(f32[3,384]{1,0:T(4,128)} %get-tuple-element.17) | copy-start | bytes 13828

commit v3 on v2

--- a/solution.py
+++ b/solution.py
@@ -12,6 +12,7 @@
 LANES = 128
 ROWS = 2
 AHEAD = 2
+SPAN = 2
 MESH = pl.DeviceIdType.MESH
 HIGHEST = lax.Precision.HIGHEST
 
@@ -124,46 +125,108 @@
     high = x.astype(jnp.bfloat16).astype(jnp.float32)
     rest = x - high
     mid = rest.astype(jnp.bfloat16).astype(jnp.float32)
-    return high, mid, rest - mid
-
-
-def force_kernel(
-    cnt_ref, tgt_ref, src_ref, out_ref, dense, src_t, spot, packed, offs
-):
+    return high, mid, (rest - mid).astype(jnp.bfloat16).astype(jnp.float32)
+
+
+def grid3(x):
+    coarse = jnp.floor(x * 8.0 + 0.5) * 0.125
+    rest = x - coarse
+    fine = jnp.floor(rest * 4096.0 + 0.5) * (1.0 / 4096.0)
+    return coarse, fine, (rest - fine).astype(jnp.bfloat16).astype(jnp.float32)
+
+
+def sum3(x):
+    return x[0:1] + x[1:2] + x[2:3]
+
+
+def levels(state):
+    xg, xm, xr = grid3(state[0:3])
+    vh, vm, vl = split3(state[3:6])
+    x, v = xg + xm + xr, vh + vm + vl
+    scalars = [
+        sum3(x * v),
+        sum3(xg * xg + 2.0 * (xg * xm)),
+        sum3(xm * xm + 2.0 * (xg * xr) + 2.0 * (xm * xr) + xr * xr),
+    ]
+    return (xg, xm, xr), (vh, vm, vl), scalars
+
+
+def source_features(state):
+    xs, vs, (s, ab, c) = levels(state)
+    one = jnp.ones_like(state[0:1])
+    none = jnp.zeros_like(one)
+    s, ab, c = split3(s), split3(ab), split3(c)
+    g = jnp.concatenate([xs[0], vs[0], s[0], one], axis=0)
+    m = jnp.concatenate([xs[1], vs[1], s[1], none], axis=0)
+    r = jnp.concatenate([xs[2], vs[2], s[2], none], axis=0)
+    e = jnp.concatenate([*ab, one, none, none, none, none], axis=0)
+    f = jnp.concatenate([*c, one, one, none, none, none], axis=0)
+    return jnp.concatenate([g, g, m, e, g, m, m, r, r, r, f, jnp.zeros_like(f)], axis=0)
+
+
+def target_features(state):
+    xs, vs, (s, ab, c) = levels(state)
+    one = jnp.ones_like(state[0:1])
+    none = jnp.zeros_like(one)
+    void = jnp.zeros_like(state[0:3])
+    zero = jnp.zeros_like(state)
+    s, ab, c = split3(s), split3(ab), split3(c + SOFTENING)
+    x2 = [-2.0 * z for z in xs]
+    xs, vs = [-z for z in xs], [-z for z in vs]
+
+    def block(*rows):
+        return jnp.concatenate(rows, axis=0)
+
+    radial = block(
+        vs[0], xs[0], one, s[0],
+        vs[1], xs[1], none, s[1],
+        vs[0], xs[0], one, none,
+        zero,
+        vs[2], xs[2], none, s[2],
+        vs[1], xs[1], none, none,
+        zero,
+        vs[0], xs[0], one, none,
+        zero, zero, zero, zero,
+    )
+    square = block(
+        x2[0], void, none, ab[0],
+        x2[1], void, none, ab[1],
+        x2[0], void, none, none,
+        one, one, one, ab[2], void, none,
+        x2[2], void, none, c[0],
+        x2[1], void, none, none,
+        x2[2], void, none, none,
+        x2[0], void, none, none,
+        x2[1], void, none, none,
+        x2[2], void, none, none,
+        one, one, one, c[1], c[2], void,
+        zero,
+    )
+    return jnp.concatenate([radial, square], axis=1).astype(jnp.bfloat16)
+
+
+def force_kernel(cnt_ref, tgt_ref, src_ref, out_ref, dense, src_t, packed, offs):
     n_a, n_b, stars = tgt_ref.shape[0], src_ref.shape[0], src_ref.shape[2]
     per = stars // LANES
     parts = n_b * per
     f32, bf16 = jnp.float32, jnp.bfloat16
     comp = lax.broadcasted_iota(jnp.int32, (8, LANES), 0)
     lane = lax.broadcasted_iota(jnp.int32, (8, LANES), 1)
-    one = jnp.ones((1, LANES), f32)
 
     def piece(j):
         b, p = j // per, j % per
         return src_ref[b, :, p * LANES : (p + 1) * LANES]
 
-    total = piece(0)
+    top = bottom = piece(0)
     for j in range(1, parts):
-        total = total + piece(j)
-    middle = jnp.sum(total, axis=1, keepdims=True) * (1.0 / (parts * LANES))
-    middle = jnp.where(comp < 6, jnp.broadcast_to(middle, (8, LANES)), 0.0)
+        top, bottom = jnp.maximum(top, piece(j)), jnp.minimum(bottom, piece(j))
+    middle = jnp.max(top, axis=1, keepdims=True) + jnp.min(bottom, axis=1, keepdims=True)
+    middle = jnp.where(comp < 6, jnp.broadcast_to(0.5 * middle, (8, LANES)), 0.0)
 
     for j in range(parts):
         state = piece(j) - middle
-        dot_xv = state[0:1] * state[3:4] + state[1:2] * state[4:5] + state[2:3] * state[5:6]
-        high, mid, low = split3(jnp.concatenate([state[3:6], state[0:3], dot_xv, one], axis=0))
-        rows = jnp.concatenate(
-            [high, mid, high, mid, low, high, state, jnp.zeros((8, LANES), f32)], axis=0
-        )
-        cols = rows.T
-        src_t[j * LANES : (j + 1) * LANES, :] = cols.astype(bf16)
-        for g in range(LANES // 8):
-            for c in range(3):
-                spot[j * (LANES // 8) + g, c] = jnp.broadcast_to(
-                    cols[8 * g : 8 * g + 8, 48 + c : 49 + c], (8, LANES)
-                )
-        mass = state[6:7]
-        moment = jnp.where(comp < 6, state * mass, jnp.where(comp == 6, state, 0.0))
+        src_t[j * LANES : (j + 1) * LANES, :] = source_features(state).T.astype(bf16)
+        moment = jnp.where(comp < 6, state * state[6:7], jnp.where(comp == 6, state, 0.0))
         high, mid, low = split3(moment)
         rows = jnp.concatenate([high, mid, low, jnp.zeros((8, LANES), f32)], axis=0).astype(bf16)
         packed[j, :, 0:LANES] = rows
@@ -182,55 +245,53 @@
 
     def tile_step(t, _):
         state = dense[t] - middle
-        dot_xv = state[0:1] * state[3:4] + state[1:2] * state[4:5] + state[2:3] * state[5:6]
-        high, mid, low = split3(jnp.concatenate([-state[0:6], one, dot_xv], axis=0))
-        pair = jnp.concatenate(
-            [high, high, mid, mid, high, low, jnp.zeros((16, LANES), f32)], axis=0
-        ).astype(bf16)
-        own = [jnp.broadcast_to(state[c : c + 1], (8, LANES)) for c in range(3)]
-
-        def radial_of(c):
-            return jnp.dot(
-                src_t[c * LANES : (c + 1) * LANES, :], pair, preferred_element_type=f32
-            )
-
-        def weights_of(c, radial):
+        pair = target_features(state)
+
+        def products_of(c):
+            left = src_t[c * SPAN * LANES : (c + 1) * SPAN * LANES, :]
+            return [
+                jnp.dot(left, pair[:, :LANES], preferred_element_type=f32),
+                jnp.dot(left, pair[:, LANES:], preferred_element_type=f32),
+            ]
+
+        def weights_of(prod, at):
             tiles_of = [[], [], [], []]
             for g in range(8):
                 pulls, twists = [], []
                 for h in range(2):
-                    at = c * 16 + 2 * g + h
-                    dx = spot[at, 0] - own[0]
-                    dy = spot[at, 1] - own[1]
-                    dz = spot[at, 2] - own[2]
-                    q = dx * dx + (dy * dy + (dz * dz + SOFTENING))
-                    inv = lax.rsqrt(q)
+                    row = slice(at + 16 * g + 8 * h, at + 16 * g + 8 * h + 8)
+                    radial = prod[0][row]
+                    inv = lax.rsqrt(prod[1][row])
                     inv2 = inv * inv
                     pull = inv * inv2
                     pulls.append(pull)
-                    twists.append((radial[16 * g + 8 * h : 16 * g + 8 * h + 8] * inv2) * pull)
+                    twists.append((radial * inv2) * pull)
                 for s, both in enumerate((pulls, twists)):
                     full = jnp.concatenate(both, axis=0)
                     high = full.astype(bf16)
                     tiles_of[s].append(high)
                     tiles_of[2 + s].append((full - high.astype(f32)).astype(bf16))
-            cols = [jnp.concatenate(x, axis=0) for x in tiles_of]
-            return jnp.concatenate(
-                [jnp.concatenate(cols[0:2], axis=1), jnp.concatenate(cols[2:4], axis=1)], axis=0
-            )
-
-        acc = jnp.zeros((32, 2 * LANES), f32)
-        ahead = [radial_of(c) for c in range(AHEAD)]
+            return [jnp.concatenate(tiles_of[s] + tiles_of[2 + s], axis=0) for s in range(2)]
+
+        acc = [jnp.zeros((32, LANES), f32)] * 2
+        groups = parts // SPAN
+        ahead = [products_of(c) for c in range(AHEAD)]
         right = None
-        for c in range(parts):
-            if c + AHEAD < parts:
-                ahead.append(radial_of(c + AHEAD))
-            last, right = right, weights_of(c, ahead[c])
-            if last is not None:
-                acc = acc + jnp.dot(packed[c - 1], last, preferred_element_type=f32)
-        acc = acc + jnp.dot(packed[parts - 1], right, preferred_element_type=f32)
-        acc = acc[0:8] + (acc[8:16] + acc[16:24])
-        pull, twist = acc[:, :LANES], acc[:, LANES:]
+        for c in range(groups):
+            if c + AHEAD < groups:
+                ahead.append(products_of(c + AHEAD))
+            for u in range(SPAN):
+                last, right = right, weights_of(ahead[c], u * LANES)
+                if last is not None:
+                    acc = [
+                        z + jnp.dot(packed[c * SPAN + u - 1], w, preferred_element_type=f32)
+                        for z, w in zip(acc, last)
+                    ]
+        acc = [
+            z + jnp.dot(packed[parts - 1], w, preferred_element_type=f32)
+            for z, w in zip(acc, right)
+        ]
+        pull, twist = [z[0:8] + (z[8:16] + z[16:24]) for z in acc]
         force = pull - state * pull[6:7]
         tide = twist - state * twist[6:7]
         jerk = force[3:6] - 3.0 * tide[0:3]
@@ -346,8 +407,7 @@
             out_specs=vmem,
             scratch_shapes=[
                 pltpu.VMEM((n_a + 2, 8, LANES), f32),
-                pltpu.VMEM((chunks * LANES, 64), jnp.bfloat16),
-                pltpu.VMEM((chunks * LANES // 8, 3, 8, LANES), f32),
+                pltpu.VMEM((chunks * LANES, 96), jnp.bfloat16),
                 pltpu.VMEM((chunks, 32, 2 * LANES), jnp.bfloat16),
                 pltpu.SMEM((n_a,), jnp.int32),
             ],

time: 58 us -> 52.4 us (0.903)
  the two profiles are of different devices: /device:TPU:33 before, /device:TPU:1 now
where the time goes in v3:
time: 52.4 us; the launch traced here: 53.1 us
  Pallas kernels  47.8 us (91%)
  local copies, waits for them, and re-layouts  3.36 us (6%)
  between operations  1.95 us (4%)
    pallas_call x1, Pallas kernels, per_device(): pl.pallas_call(functools.partial(exchange_kernel, n_row, n_col, strength)...  18.9 us
    pallas_call x1, Pallas kernels, per_device(): pl.pallas_call(force_kernel, out_shape=jax.ShapeDtypeStruct((n_a, 8, LANE...  17.4 us
    pallas_call x1, Pallas kernels, per_device(): pl.pallas_call(functools.partial(return_kernel, n_row, n_col), out_shape=...  11.5 us
    unnamed x12, local copies, waits for them, and re-layouts  3.36 us

profile of v3, /device:TPU:1, one launch (start us, length us, event | category | flops | bytes accessed | tf_op | source)
XLA Modules:
  0.0 53.1 jit_solution(8552148394931797378)
XLA Ops:
  1.9 18.9 %exchange.1 = (f32[32,8,128]{2,1,0:T(8,128)}, f32[8,8,384]{2,1,0:T(8,128)}, s32[1,128]{1,0:T(1,128)}) custom-call(f32[1]{0:T(128)S(6)} %copy.17.step_ref, s32[1,1]{1,0:T(1,128)S(6)} %copy.18.count_ref, f32[3,384]{1,0:T(4,128)} %pos_ref.3, f32[3,384]{1,0:T(4,128)} %vel_ref.3, f32[3,384]{1,0:T(4,128)} %acc_ref.3, f32[3,384]{1,0:T(4,128)} %jerk_ref.3, ...), custom_call_target="tpu_custom_call" | custom-call | tf_op jit(solution)/shard_map/exchange/pallas_call | solution.py:384
  20.8 17.4 %forces.1.part_ref = f32[32,8,128]{2,1,0:T(8,128)} custom-call(s32[1,128]{1,0:T(1,128)} %get-tuple-element.7.cnt_ref, f32[32,8,128]{2,1,0:T(8,128)} %get-tuple-element.8.tgt_ref, f32[8,8,384]{2,1,0:T(8,128)} %get-tuple-element.9.src_ref), custom_call_target="tpu_custom_call" | custom-call | tf_op jit(solution)/shard_map/forces/pallas_call | solution.py:403
  38.2 11.5 %returns.1 = (f32[3,384]{1,0:T(4,128)}, f32[3,384]{1,0:T(4,128)}, f32[3,384]{1,0:T(4,128)}, f32[3,384]{1,0:T(4,128)}) custom-call(f32[1]{0:T(128)S(6)} %copy.17.step_ref, s32[1,1]{1,0:T(1,128)S(6)} %copy.18.count_ref, f32[32,8,128]{2,1,0:T(8,128)} %forces.1.part_ref, f32[3,384]{1,0:T(4,128)} %pos_ref.3, f32[3,384]{1,0:T(4,128)} %vel_ref.3, ...), custom_call_target="tpu_custom_call" | custom-call | tf_op jit(solution)/shard_map/returns/pallas_call | solution.py:416
  49.7 0.0 copy-start.3
  49.8 0.7 %copy-done.3 = f32[3,384]{1,0:T(4,128)S(1)} copy-done((f32[3,384]{1,0:T(4,128)S(1)}, f32[3,384]{1,0:T(4,128)}, u32[]{:S(2)}) %copy-start.3) | copy-done | bytes 4632
  50.4 0.0 copy-start.2
  50.4 0.6 %copy.19 = f32[3,384]{1,0:T(4,128)} copy(f32[3,384]{1,0:T(4,128)S(1)} %copy-done.3) | data formatting | bytes 9216
  51.0 0.1 copy-done.2
  51.1 0.0 copy-start.1
  51.1 0.6 %copy.20 = f32[3,384]{1,0:T(4,128)} copy(f32[3,384]{1,0:T(4,128)S(1)} %copy-done.2) | data formatting | bytes 9216
  51.7 0.1 copy-done.1
  51.8 0.0 copy-start
  51.8 0.6 %copy.21 = f32[3,384]{1,0:T(4,128)} copy(f32[3,384]{1,0:T(4,128)S(1)} %copy-done.1) | data formatting | bytes 9216
  52.4 0.1 copy-done
  52.5 0.6 %copy.22 = f32[3,384]{1,0:T(4,128)} copy(f32[3,384]{1,0:T(4,128)S(1)} %copy-done) | data formatting | bytes 9216
Async XLA Ops:
  49.7 0.7 %copy-start.3 = (f32[3,384]{1,0:T(4,128)S(1)}, f32[3,384]{1,0:T(4,128)}, u32[]{:S(2)}) copy-start(f32[3,384]{1,0:T(4,128)} %get-tuple-element.14) | copy-start | bytes 13828
  50.4 0.7 %copy-start.2 = (f32[3,384]{1,0:T(4,128)S(1)}, f32[3,384]{1,0:T(4,128)}, u32[]{:S(2)}) copy-start(f32[3,384]{1,0:T(4,128)} %get-tuple-element.15) | copy-start | bytes 13828
  51.1 0.7 %copy-start.1 = (f32[3,384]{1,0:T(4,128)S(1)}, f32[3,384]{1,0:T(4,128)}, u32[]{:S(2)}) copy-start(f32[3,384]{1,0:T(4,128)} %get-tuple-element.16) | copy-start | bytes 13828
  51.8 0.7 %copy-start = (f32[3,384]{1,0:T(4,128)S(1)}, f32[3,384]{1,0:T(4,128)}, u32[]{:S(2)}) copy-start(f32[3,384]{1,0:T(4,128)} %get-tuple-element.17) | copy-start | bytes 13828
